TPU v7x, 32 devices: a whole 2x2x4 slice. The times are simulated.
32 devices in a mesh: seq: 4 (over z), mp: 8 (over y, x, core).
Axes of the slice: x: 2, y: 2, z: 4, core: 2. Of those that a mesh axis runs over, the one named last changes fastest.
Arguments:
- enc_rows: bfloat16 [1024, 1024], P('seq', 'mp'), may hold values from -6 to 6
- ffn_in: bfloat16 [1024, 65536], P('seq', 'mp'), may hold values from -0.1875 to 0.1875
- ffn_out: bfloat16 [65536, 1024], P('mp', 'seq'), may hold values from -0.03125 to 0.03125
- enc_gain: float32 [1024], replicated, may hold values from 0.25 to 1.75
- final_gain: float32 [1024], replicated, may hold values from 0.25 to 1.75
- sent_lengths: int32 [4, 4], replicated, may hold values from 1 to 128, 256 in all within a row
- group_table: int32 [4, 4], replicated, may hold values from 0 to 3, as said below
- dec_rows: bfloat16 [1024, 1024], P('seq', 'mp'), may hold values from -6 to 6
- dec_gain: float32 [2, 1024], replicated, may hold values from 0.25 to 1.75
- w_query: bfloat16 [2, 1024, 8192], P(None, None, 'mp'), may hold values from -0.1875 to 0.1875
- w_key: bfloat16 [2, 1024, 8192], P(None, None, 'mp'), may hold values from -0.1875 to 0.1875
- w_value: bfloat16 [2, 1024, 8192], P(None, None, 'mp'), may hold values from -0.1875 to 0.1875
- w_output: bfloat16 [2, 8192, 1024], P(None, 'mp'), may hold values from -0.0625 to 0.0625
Outputs:
- dec_out: bfloat16 [1024, 1024], P('seq', 'mp')
Inputs may be any that keep to these rules, and one draw needn't show every extreme that they name: `sent_lengths`: each row sums to 256; each row has an entry equal to 128. `group_table`: every row and every column holds each group number exactly once.
All inputs are finite; a program needn't handle non-finite values.
Results may differ from a plain program's by a relative error of at most 0.014.
Values may be sent and summed in bfloat16 or wider, within the bound.
A program may use at most 128 MiB of HBM per device.

v0:
```python
import jax
import jax.numpy as jnp
from jax import lax
from jax.sharding import PartitionSpec as P

D = 1024
DH = 128
LAYERS = 2


epsilon = 1e-06


def rms_scale(values, gain_row):
    mean_square = jnp.mean(values * values, axis=-1, keepdims=True)
    return values * lax.rsqrt(mean_square + epsilon) * gain_row


def shards(
    enc_rows,
    ffn_in,
    ffn_out,
    enc_gain,
    final_gain,
    sent_lengths,
    group_table,
    dec_rows,
    dec_gain,
    w_query,
    w_key,
    w_value,
    w_output,
):
    group_count = lax.axis_size("seq")
    my_group = lax.axis_index("seq")
    col_width = enc_rows.shape[1]
    col_start = lax.axis_index("mp") * col_width
    row_count = enc_rows.shape[0]
    max_length = 2 * row_count // group_count
    whole_rows = lax.all_gather(enc_rows, "mp", axis=1, tiled=True)
    normed = rms_scale(whole_rows.astype(jnp.float32), enc_gain).astype(jnp.bfloat16)
    full_in = lax.all_gather(ffn_in, "seq", axis=0, tiled=True)
    inner = jnp.dot(normed, full_in, preferred_element_type=jnp.float32)
    hidden = jnp.maximum(inner, 0.0).astype(jnp.bfloat16)
    partial_out = jnp.dot(
        hidden,
        lax.all_gather(ffn_out, "seq", axis=1, tiled=True),
        preferred_element_type=jnp.float32,
    )
    my_lengths = lax.dynamic_index_in_dim(sent_lengths, my_group, 0, keepdims=False)
    my_targets = lax.dynamic_index_in_dim(group_table, my_group, 0, keepdims=False)
    my_starts = jnp.cumsum(my_lengths) - my_lengths
    group_ids = jnp.arange(group_count, dtype=jnp.int32)
    matches = my_targets[None, :] == group_ids[:, None]
    send_starts = jnp.sum(jnp.where(matches, my_starts[None, :], 0), axis=1)
    positions = jnp.arange(max_length, dtype=jnp.int32)
    row_index = jnp.minimum(send_starts[:, None] + positions[None, :], row_count - 1)
    recv_lengths = jnp.sum(jnp.where(group_table == my_group, sent_lengths, 0), axis=1)
    live_mask = positions[None, :] < recv_lengths[:, None]
    kv_width = w_key.shape[2]
    weight_list = []
    for layer_index in range(LAYERS):
        weight_list.append(w_key[layer_index])
        weight_list.append(w_value[layer_index])
    enc_share = lax.psum_scatter(partial_out, "mp", scatter_dimension=1, tiled=True)
    encoded = enc_rows.astype(jnp.float32) + enc_share
    squares = lax.psum(jnp.sum(encoded * encoded, axis=1), "mp")
    gain_part = lax.dynamic_slice_in_dim(final_gain, col_start, col_width, 0)
    memory = (encoded * lax.rsqrt(squares / D + epsilon)[:, None] * gain_part).astype(jnp.bfloat16)
    blocks = memory[row_index]
    gathered = lax.all_gather(
        lax.all_to_all(blocks, "seq", split_axis=0, concat_axis=0, tiled=True),
        "mp",
        axis=2,
        tiled=True,
    )
    projected = tuple(
        (
            jnp.einsum(
                "std,de->ste", gathered, weight_matrix, preferred_element_type=jnp.float32
            ).astype(jnp.bfloat16)
            for weight_matrix in weight_list
        )
    )
    tgt_rows = dec_rows.shape[0]
    per_sentence = tgt_rows // group_count
    local_heads = kv_width // DH
    final_state = dec_rows.astype(jnp.float32)
    for layer_index in range(LAYERS):
        state_half = lax.all_gather(final_state.astype(jnp.bfloat16), "mp", axis=1, tiled=True)
        normed_rows = rms_scale(state_half.astype(jnp.float32), dec_gain[layer_index]).astype(
            jnp.bfloat16
        )
        queries = (
            jnp.dot(normed_rows, w_query[layer_index], preferred_element_type=jnp.float32)
            * DH ** (-0.5)
        ).astype(jnp.bfloat16)
        query_heads = queries.reshape(group_count, per_sentence, local_heads, DH)
        key_heads = projected[2 * layer_index].reshape(group_count, max_length, local_heads, DH)
        value_heads = projected[2 * layer_index + 1].reshape(
            group_count, max_length, local_heads, DH
        )
        scores = jnp.einsum(
            "sqhd,sthd->shqt", query_heads, key_heads, preferred_element_type=jnp.float32
        )
        scores = jnp.where(live_mask[:, None, None, :], scores, -jnp.inf)
        weights = jax.nn.softmax(scores, axis=-1).astype(jnp.bfloat16)
        attended = jnp.einsum(
            "shqt,sthd->sqhd", weights, value_heads, preferred_element_type=jnp.float32
        ).astype(jnp.bfloat16)
        final_state = final_state + lax.psum_scatter(
            jnp.dot(
                attended.reshape(tgt_rows, kv_width),
                w_output[layer_index],
                preferred_element_type=jnp.float32,
            ).astype(jnp.bfloat16),
            "mp",
            scatter_dimension=1,
            tiled=True,
        ).astype(jnp.float32)
    return final_state.astype(jnp.bfloat16)


def solution(mesh):
    in_specs = (
        P("seq", "mp"),
        P("seq", "mp"),
        P("mp", "seq"),
        P(),
        P(),
        P(),
        P(),
        P("seq", "mp"),
        P(),
        P(None, None, "mp"),
        P(None, None, "mp"),
        P(None, None, "mp"),
        P(None, "mp", None),
    )
    out_specs = P("seq", "mp")
    return jax.shard_map(shards, mesh=mesh, in_specs=in_specs, out_specs=out_specs, check_vma=False)
```

profile of v0, /device:TPU:0, one launch (start us, length us, event | category | flops | bytes accessed | tf_op | source)
XLA Modules:
  0.0 798.2 jit_solution(7540676980709802126)
XLA Ops:
  6.5 0.7 all-gather.6.cloned.1.call-update
  7.3 0.7 all-gather.4.cloned.1.call-update
  8.1 11.5 %all_gather.18 = bf16[256,1024]{1,0:T(8,128)(2,1)S(1)} all-gather(bf16[256,128]{1,0:T(8,128)(2,1)S(1)} %copy-done), channel_id=1, replica_groups=mesh['seq'=4,'mp'=8] {'mp'}, dimensions={1}, use_global_device_ids=true | all-gather | bytes 589824 | tf_op jit(solution)/shard_map/all_gather | solution.py:40
  19.5 0.2 fusion.81
  19.8 278.1 %all-gather.6.cloned.1.call-done = bf16[8192,1024]{1,0:T(8,128)(2,1)} async-done(((bf16[8192,256]{1,0:T(8,128)(2,1)}), bf16[8192,1024]{1,0:T(8,128)(2,1)}) %all-gather.6.cloned.1.call-update) | async-done | bytes 16777232 | tf_op jit(solution)/shard_map/all_gather | solution.py:47
  297.9 286.5 %all-gather.4.cloned.1.call-done = bf16[1024,8192]{1,0:T(8,128)(2,1)} async-done(((bf16[256,8192]{1,0:T(8,128)(2,1)}), bf16[1024,8192]{1,0:T(8,128)(2,1)}) %all-gather.4.cloned.1.call-update) | async-done | bytes 16777232 | tf_op jit(solution)/shard_map/all_gather | solution.py:42
  584.4 16.1 %fusion.98 = f32[256,1024]{1,0:T(8,128)} fusion(bf16[8192,1024]{1,0:T(8,128)(2,1)} %all-gather.6.cloned.1.call-done, bf16[1024,8192]{1,0:T(8,128)(2,1)} %all-gather.4.cloned.1.call-done, bf16[256,1024]{1,0:T(8,128)(2,1)S(1)} %all_gather.18, f32[1024]{0:T(1024)S(1)} %copy-done.8, f32[256]{0:T(256)S(1)} %add_rsqrt_fusion.3), kind=kOutput, calls=%fused_computation.80 | convolution fusion | flops 8595177472 | bytes 35132416 | tf_op jit(solution)/shard_map/dot_general | solution.py:45
  600.7 0.2 reduce-window_clone.1
  600.8 0.8 dynamic_slice.10
  601.6 0.1 select_reduce_fusion.1
  601.7 0.1 fusion.120
  601.8 33.1 %reduce-scatter.8.cloned.1.call-done = f32[256,128]{1,0:T(8,128)} async-done(((f32[256,1024]{1,0:T(8,128)}), f32[256,128]{1,0:T(8,128)}) %reduce-scatter.8.cloned.1.call-update) | async-done | bytes 131088 | tf_op jit(solution)/shard_map/reduce_scatter | solution.py:65
  634.9 1.0 multiply_reduce_fusion
  635.9 12.3 %psum.7 = f32[256]{0:T(256)S(1)} all-reduce(f32[256]{0:T(256)S(1)} %multiply_reduce_fusion), channel_id=1, replica_groups=mesh['seq'=4,'mp'=8] {'mp'}, use_global_device_ids=true, to_apply=%region_3.4 | all-reduce | flops 256 | bytes 2048 | tf_op jit(solution)/shard_map/psum | solution.py:67
  648.2 1.0 multiply_convert_fusion
  649.3 1.3 gather_fusion
  650.6 10.4 %all_to_all.5 = bf16[4,128,128]{2,1,0:T(8,128)(2,1)} all-to-all(bf16[4,128,128]{2,1,0:T(8,128)(2,1)S(1)} %bitcast.129), channel_id=1, replica_groups=mesh['seq'=4,'mp'=8] {'seq'}, dimensions={0} | all-to-all | bytes 262144 | tf_op jit(solution)/shard_map/all_to_all | solution.py:72
  661.1 11.2 %all_gather.22 = bf16[256,1024]{1,0:T(8,128)(2,1)S(1)} all-gather(bf16[256,128]{1,0:T(8,128)(2,1)S(1)} %copy-done.1), channel_id=1, replica_groups=mesh['seq'=4,'mp'=8] {'mp'}, dimensions={1}, use_global_device_ids=true | all-gather | bytes 589824 | tf_op jit(solution)/shard_map/all_gather | solution.py:90
  672.4 0.2 fusion.84
  672.6 2.4 fusion.73
  675.0 0.1 copy.44
  675.1 0.1 select_reduce_fusion
  675.3 7.7 all-gather.8.cloned.1.call-done
  682.9 3.3 fusion.49
  686.2 0.8 convolution_select_fusion.1
  687.1 0.6 fusion.125
  687.7 2.3 fusion.52
  690.0 4.8 fusion.79
  694.8 0.3 copy.31
  695.2 2.3 fusion.61
  697.5 1.0 copy.36
  698.6 4.0 fusion.46
  702.6 1.3 fusion.43
  703.9 28.9 %reduce-scatter.10.cloned.1.call-done = bf16[128,256]{1,0:T(8,128)(2,1)} async-done(((bf16[1024,256]{1,0:T(8,128)(2,1)}), bf16[128,256]{1,0:T(8,128)(2,1)}) %reduce-scatter.10.cloned.1.call-update) | async-done | bytes 65552
  732.8 0.9 copy.37
  733.8 10.2 %all_gather.23 = bf16[256,1024]{1,0:T(8,128)(2,1)S(1)} all-gather(bf16[256,128]{1,0:T(8,128)(2,1)S(1)} %fusion.119), channel_id=1, replica_groups=mesh['seq'=4,'mp'=8] {'mp'}, dimensions={1}, use_global_device_ids=true | all-gather | bytes 589824 | tf_op jit(solution)/shard_map/all_gather | solution.py:90
  743.9 0.2 fusion.87
  744.1 2.5 fusion.76
  746.6 0.1 copy.46
  746.7 0.8 convolution_select_fusion
  747.5 0.6 fusion.126
  748.2 3.6 fusion.80
  751.8 0.3 copy.35
  752.2 2.3 fusion.64
  754.5 1.0 copy.38
  755.5 34.3 %reduce-scatter.12.cloned.1.call-done = bf16[128,256]{1,0:T(8,128)(2,1)} async-done(((bf16[1024,256]{1,0:T(8,128)(2,1)}), bf16[128,256]{1,0:T(8,128)(2,1)}) %reduce-scatter.12.cloned.1.call-update) | async-done | bytes 65552
  789.7 0.9 copy.39
  790.7 0.7 add_convert_fusion
  (40 shorter events, 0.5 us)
Async XLA Ops:
  6.5 1.5 copy-start
  6.5 577.9 %copy-start.8 = (f32[1024]{0:T(1024)S(1)}, f32[1024]{0:T(1024)}, u32[]{:S(2)}) copy-start(f32[1024]{0:T(1024)} %param.16) | copy-start | bytes 12292
  6.5 291.4 %all-gather.6.cloned.1.call-start = ((), (), s32[]{:S(2)}) async-start(), calls=%async_computation.5 | async-start | bytes 20971520 | tf_op jit(solution)/shard_map/all_gather | solution.py:47
  7.3 577.2 %all-gather.4.cloned.1.call-start = ((), (), s32[]{:S(2)}) async-start(), calls=%async_computation.4 | async-start | bytes 20971520 | tf_op jit(solution)/shard_map/all_gather | solution.py:42
  8.0 626.9 %reduce-scatter.8.cloned.1.call-start = ((), (), s32[]{:S(2)}) async-start(), calls=%async_computation.6 | async-start | bytes 1179648 | tf_op jit(solution)/shard_map/reduce_scatter | solution.py:65
  19.7 580.9 %copy-start.3 = (s32[4,4]{1,0:T(4,128)S(1)}, s32[4,4]{1,0:T(4,128)}, u32[]{:S(2)}) copy-start(s32[4,4]{1,0:T(4,128)} %param.18) | copy-start | bytes 196
  19.7 581.9 %copy-start.4 = (s32[4,4]{1,0:T(4,128)S(1)}, s32[4,4]{1,0:T(4,128)}, u32[]{:S(2)}) copy-start(s32[4,4]{1,0:T(4,128)} %param.19) | copy-start | bytes 196
  19.7 641.4 %copy-start.1 = (bf16[256,128]{1,0:T(8,128)(2,1)S(1)}, bf16[256,128]{1,0:T(8,128)(2,1)}, u32[]{:S(2)}) copy-start(bf16[256,128]{1,0:T(8,128)(2,1)} %param.20) | copy-start | bytes 196612
  600.6 72.0 %copy-start.2 = (f32[2,1024]{1,0:T(2,128)S(1)}, f32[2,1024]{1,0:T(2,128)}, u32[]{:S(2)}) copy-start(f32[2,1024]{1,0:T(2,128)} %param.21) | copy-start | bytes 24580
  600.6 82.3 %all-gather.8.cloned.1.call-start = ((), (), s32[]{:S(2)}) async-start(), calls=%async_computation.7 | async-start | bytes 1179648 | tf_op jit(solution)/shard_map/all_gather | solution.py:71
  661.1 71.7 %reduce-scatter.10.cloned.1.call-start = ((), (), s32[]{:S(2)}) async-start(), calls=%async_computation.8 | async-start | bytes 589824
  682.9 4.8 copy-start.5
  682.9 4.8 copy-start.7
  698.5 91.2 %reduce-scatter.12.cloned.1.call-start = ((), (), s32[]{:S(2)}) async-start(), calls=%async_computation.9 | async-start | bytes 589824
  698.6 4.0 copy-start.6
  744.1 4.0 copy-start.9
Sparse Core Ops, SparseCore 0:
  8.9 288.9 all-gather.5
  299.5 284.9 all-gather.3
  600.7 34.1 reduce-scatter.7
  661.2 21.6 all-gather.7
  698.6 34.1 reduce-scatter.9
  755.6 34.0 reduce-scatter.11
where the time goes:
time: 799 us; the launch traced here: 798 us
  waiting for transfers between devices  670 us (84%)
  blocking collectives  55.6 us (7%)
  matrix products  46.5 us (6%)
  between operations  13.7 us (2%)
    all_gather x1, waiting for transfers between devices, shards(): full_in = lax.all_gather(ffn_in, 'seq', axis=0, tiled=True)  287 us
    all_gather x1, waiting for transfers between devices, shards(): lax.all_gather(ffn_out, 'seq', axis=1, tiled=True)  278 us
    unnamed x8, waiting for transfers between devices  64.7 us
    reduce_scatter x1, waiting for transfers between devices, shards(): lax.psum_scatter(partial_out, 'mp', scatter_dimension=1, tiled=True)  33.1 us
    all_gather x2, blocking collectives, shards(): lax.all_gather(final_state.astype(jnp.bfloat16), 'mp', axis=1, tiled=True)  21.4 us
    dot_general x1, matrix products, shards(): jnp.dot(hidden, lax.all_gather(ffn_out, 'seq', axis=1, tiled=True), prefe...  16.1 us
  transfers between devices with their start and end apart: 6, of which 6 were waited for; matrix products, arithmetic and copies ran while one was open for 1% of the time, Pallas kernels for 0%

commit v1 on v0

--- a/solution.py
+++ b/solution.py
@@ -1,7 +1,13 @@
+import functools
+
 import jax
 import jax.numpy as jnp
 from jax import lax
+from jax.experimental import pallas as pl
+from jax.experimental.pallas import tpu as pltpu
 from jax.sharding import PartitionSpec as P
+
+MESH = pl.DeviceIdType.MESH
 
 D = 1024
 DH = 128
@@ -14,6 +20,314 @@
 def rms_scale(values, gain_row):
     mean_square = jnp.mean(values * values, axis=-1, keepdims=True)
     return values * lax.rsqrt(mean_square + epsilon) * gain_row
+
+
+def flip(index, bits):
+    out = index
+    for power in (1, 2, 4, 8, 16, 32):
+        if bits & power:
+            out = out + power - 2 * power * ((out // power) % 2)
+    return out
+
+
+def z_order(count):
+    return sorted(range(1, count), key=lambda bits: (bits == 1, bits))
+
+
+def ffn_kernel(
+    n_seq,
+    n_mp,
+    enc_ref,
+    gain_ref,
+    fin_ref,
+    fout_ref,
+    share_ref,
+    enc_all,
+    normed,
+    win,
+    wout,
+    hidden,
+    part_out,
+    part_in,
+    z_out,
+    z_in,
+    enc_zs,
+    enc_zr,
+    enc_ps,
+    enc_pr,
+    in_s,
+    in_r,
+    out_s,
+    out_r,
+    red_ps,
+    red_pr,
+    red_zs,
+    red_zr,
+    local_sem,
+):
+    s = lax.axis_index("seq")
+    m = lax.axis_index("mp")
+    rows, width = enc_ref.shape
+    depth = fin_ref.shape[0]
+    units = fin_ref.shape[1] // n_seq
+    out_width = fout_ref.shape[1]
+    total_rows = rows * n_seq
+    per_block = out_width // width
+
+    barrier = pltpu.get_barrier_semaphore()
+    for bits in range(1, n_seq):
+        pl.semaphore_signal(barrier, inc=1, device_id=(flip(s, bits), m), device_id_type=MESH)
+    for bits in range(1, n_mp):
+        pl.semaphore_signal(barrier, inc=1, device_id=(s, flip(m, bits)), device_id_type=MESH)
+    pl.semaphore_wait(barrier, n_seq + n_mp - 2)
+
+    my_rows = pl.ds(pl.multiple_of(s * rows, rows), rows)
+
+    own_enc = pltpu.make_async_copy(enc_ref, enc_all.at[m, my_rows], local_sem.at[0])
+    own_enc.start()
+    enc_z = []
+    for bits in z_order(n_seq):
+        copy = pltpu.make_async_remote_copy(
+            src_ref=enc_ref,
+            dst_ref=enc_all.at[m, my_rows],
+            send_sem=enc_zs.at[bits],
+            recv_sem=enc_zr.at[bits],
+            device_id=(flip(s, bits), m),
+            device_id_type=MESH,
+        )
+        copy.start()
+        enc_z.append(copy)
+
+    own_in = pltpu.make_async_copy(
+        fin_ref.at[:, pl.ds(pl.multiple_of(s * units, units), units)], win.at[s], local_sem.at[1]
+    )
+    own_in.start()
+    own_out = pltpu.make_async_copy(
+        fout_ref.at[pl.ds(pl.multiple_of(s * units, units), units)], wout.at[s], local_sem.at[2]
+    )
+    own_out.start()
+    in_copies = []
+    out_copies = []
+    for bits in z_order(n_seq):
+        peer = flip(s, bits)
+        copy = pltpu.make_async_remote_copy(
+            src_ref=fin_ref.at[:, pl.ds(pl.multiple_of(peer * units, units), units)],
+            dst_ref=win.at[s],
+            send_sem=in_s.at[bits],
+            recv_sem=in_r.at[bits],
+            device_id=(peer, m),
+            device_id_type=MESH,
+        )
+        copy.start()
+        in_copies.append(copy)
+    for bits in z_order(n_seq):
+        peer = flip(s, bits)
+        copy = pltpu.make_async_remote_copy(
+            src_ref=fout_ref.at[pl.ds(pl.multiple_of(peer * units, units), units)],
+            dst_ref=wout.at[s],
+            send_sem=out_s.at[bits],
+            recv_sem=out_r.at[bits],
+            device_id=(peer, m),
+            device_id_type=MESH,
+        )
+        copy.start()
+        out_copies.append(copy)
+
+    own_enc.wait()
+    for copy in enc_z:
+        copy.wait()
+
+    enc_p = []
+    for bits in range(1, n_mp):
+        copy = pltpu.make_async_remote_copy(
+            src_ref=enc_all.at[m],
+            dst_ref=enc_all.at[m],
+            send_sem=enc_ps.at[bits],
+            recv_sem=enc_pr.at[bits],
+            device_id=(s, flip(m, bits)),
+            device_id_type=MESH,
+        )
+        copy.start()
+        enc_p.append(copy)
+    for copy in enc_p:
+        copy.wait()
+
+    chunk = min(256, rows)
+
+    def norm_chunk(i, carry):
+        span = pl.ds(pl.multiple_of(i * chunk, chunk), chunk)
+        squares = jnp.zeros((chunk, 1), jnp.float32)
+        for k in range(n_mp):
+            value = enc_all[k, span, :].astype(jnp.float32)
+            squares = squares + jnp.sum(value * value, axis=1, keepdims=True)
+        scale = lax.rsqrt(squares / (n_mp * width) + epsilon)
+        for k in range(n_mp):
+            cols = pl.ds(k * width, width)
+            value = enc_all[k, span, :].astype(jnp.float32)
+            normed[span, cols] = (value * scale * gain_ref[:, cols]).astype(jnp.bfloat16)
+        return carry
+
+    lax.fori_loop(0, total_rows // chunk, norm_chunk, 0)
+
+    own_in.wait()
+    for copy in in_copies:
+        copy.wait()
+
+    tile = min(256, units)
+
+    def hidden_chunk(i, carry):
+        cols = pl.ds(pl.multiple_of((i % (units // tile)) * tile, tile), tile)
+        span = pl.ds(pl.multiple_of((i // (units // tile)) * chunk, chunk), chunk)
+        acc = jnp.zeros((chunk, tile), jnp.float32)
+        for k in range(n_seq):
+            acc = acc + jnp.dot(
+                normed[span, pl.ds(k * depth, depth)],
+                win[k, :, cols],
+                preferred_element_type=jnp.float32,
+            )
+        hidden[span, cols] = jnp.maximum(acc, 0.0).astype(jnp.bfloat16)
+        return carry
+
+    lax.fori_loop(0, (total_rows // chunk) * (units // tile), hidden_chunk, 0)
+
+    own_out.wait()
+
+    def out_block(block):
+        def rows_chunk(i, carry):
+            span = pl.ds(pl.multiple_of(i * chunk, chunk), chunk)
+            value = jnp.dot(hidden[span, :], wout[block], preferred_element_type=jnp.float32)
+            for j in range(per_block):
+                part_out[block * per_block + j, span, :] = value[
+                    :, j * width : (j + 1) * width
+                ].astype(jnp.bfloat16)
+            return carry
+
+        lax.fori_loop(0, total_rows // chunk, rows_chunk, 0)
+
+    def send_copy(slot):
+        return pltpu.make_async_remote_copy(
+            src_ref=part_out.at[slot],
+            dst_ref=part_in.at[m],
+            send_sem=red_ps.at[slot],
+            recv_sem=red_pr.at[m],
+            device_id=(s, slot),
+            device_id_type=MESH,
+        )
+
+    def send_block(block):
+        out_block(block)
+        for j in range(per_block):
+            slot = block * per_block + j
+
+            @pl.when(slot != m)
+            def _():
+                send_copy(slot).start()
+
+    send_block(s)
+    for bits, copy in zip(z_order(n_seq), out_copies):
+        copy.wait()
+        send_block(flip(s, bits))
+
+    for bits in range(1, n_mp):
+        send_copy(flip(m, bits)).wait_send()
+    for bits in range(1, n_mp):
+        peer = flip(m, bits)
+        pltpu.make_async_remote_copy(
+            src_ref=part_out.at[peer],
+            dst_ref=part_in.at[peer],
+            send_sem=red_ps.at[peer],
+            recv_sem=red_pr.at[peer],
+            device_id=(s, peer),
+            device_id_type=MESH,
+        ).wait_recv()
+
+    def reduce_rows(block):
+        span = pl.ds(pl.multiple_of(block * rows, rows), rows)
+        total = part_out[m, span, :].astype(jnp.float32)
+        for bits in range(1, n_mp):
+            total = total + part_in[flip(m, bits), span, :].astype(jnp.float32)
+        return total
+
+    red_z = []
+    for bits in z_order(n_seq):
+        peer = flip(s, bits)
+        z_out[bits] = reduce_rows(peer).astype(jnp.bfloat16)
+        copy = pltpu.make_async_remote_copy(
+            src_ref=z_out.at[bits],
+            dst_ref=z_in.at[bits],
+            send_sem=red_zs.at[bits],
+            recv_sem=red_zr.at[bits],
+            device_id=(peer, m),
+            device_id_type=MESH,
+        )
+        copy.start()
+        red_z.append(copy)
+    total = reduce_rows(s)
+    for bits, copy in zip(z_order(n_seq), red_z):
+        copy.wait()
+        total = total + z_in[bits].astype(jnp.float32)
+    share_ref[...] = enc_ref[...].astype(jnp.float32) + total
+
+
+def ffn_fast(enc_rows, ffn_in, ffn_out, enc_gain):
+    n_seq, n_mp = lax.axis_size("seq"), lax.axis_size("mp")
+    rows, width = enc_rows.shape
+    depth, units = ffn_in.shape[0], ffn_in.shape[1] // n_seq
+    out_width = ffn_out.shape[1]
+    total = rows * n_seq
+    full = width * n_mp
+    dma = pltpu.SemaphoreType.DMA
+    return pl.pallas_call(
+        functools.partial(ffn_kernel, n_seq, n_mp),
+        out_shape=jax.ShapeDtypeStruct((rows, width), jnp.float32),
+        in_specs=[
+            pl.BlockSpec(memory_space=pltpu.VMEM),
+            pl.BlockSpec(memory_space=pltpu.VMEM),
+            pl.BlockSpec(memory_space=pl.ANY),
+            pl.BlockSpec(memory_space=pl.ANY),
+        ],
+        out_specs=pl.BlockSpec(memory_space=pltpu.VMEM),
+        scratch_shapes=[
+            pltpu.VMEM((n_mp, total, width), jnp.bfloat16),
+            pltpu.VMEM((total, full), jnp.bfloat16),
+            pltpu.VMEM((n_seq, depth, units), jnp.bfloat16),
+            pltpu.VMEM((n_seq, units, out_width), jnp.bfloat16),
+            pltpu.VMEM((total, units), jnp.bfloat16),
+            pltpu.VMEM((n_mp, total, width), jnp.bfloat16),
+            pltpu.VMEM((n_mp, total, width), jnp.bfloat16),
+            pltpu.VMEM((n_seq, rows, width), jnp.bfloat16),
+            pltpu.VMEM((n_seq, rows, width), jnp.bfloat16),
+            dma((n_seq,)),
+            dma((n_seq,)),
+            dma((n_mp,)),
+            dma((n_mp,)),
+            dma((n_seq,)),
+            dma((n_seq,)),
+            dma((n_seq,)),
+            dma((n_seq,)),
+            dma((n_mp,)),
+            dma((n_mp,)),
+            dma((n_seq,)),
+            dma((n_seq,)),
+            dma((3,)),
+        ],
+        compiler_params=pltpu.CompilerParams(
+            collective_id=0, has_side_effects=True, vmem_limit_bytes=48 * 1024 * 1024
+        ),
+    )(enc_rows, enc_gain.reshape(1, full), ffn_in, ffn_out)
+
+
+def fast_shapes(enc_rows, ffn_in, ffn_out):
+    n_seq, n_mp = lax.axis_size("seq"), lax.axis_size("mp")
+    power = (n_seq & (n_seq - 1)) == 0 and (n_mp & (n_mp - 1)) == 0
+    aligned = (
+        enc_rows.shape[1] % 128 == 0
+        and ffn_in.shape[0] % 128 == 0
+        and (ffn_in.shape[1] // n_seq) % 256 == 0
+        and ffn_out.shape[1] % enc_rows.shape[1] == 0
+        and enc_rows.shape[0] % 256 == 0
+    )
+    return power and aligned
 
 
 def shards(
@@ -37,16 +351,20 @@
     col_start = lax.axis_index("mp") * col_width
     row_count = enc_rows.shape[0]
     max_length = 2 * row_count // group_count
-    whole_rows = lax.all_gather(enc_rows, "mp", axis=1, tiled=True)
-    normed = rms_scale(whole_rows.astype(jnp.float32), enc_gain).astype(jnp.bfloat16)
-    full_in = lax.all_gather(ffn_in, "seq", axis=0, tiled=True)
-    inner = jnp.dot(normed, full_in, preferred_element_type=jnp.float32)
-    hidden = jnp.maximum(inner, 0.0).astype(jnp.bfloat16)
-    partial_out = jnp.dot(
-        hidden,
-        lax.all_gather(ffn_out, "seq", axis=1, tiled=True),
-        preferred_element_type=jnp.float32,
-    )
+    fast = fast_shapes(enc_rows, ffn_in, ffn_out)
+    if fast:
+        encoded = ffn_fast(enc_rows, ffn_in, ffn_out, enc_gain)
+    else:
+        whole_rows = lax.all_gather(enc_rows, "mp", axis=1, tiled=True)
+        normed = rms_scale(whole_rows.astype(jnp.float32), enc_gain).astype(jnp.bfloat16)
+        full_in = lax.all_gather(ffn_in, "seq", axis=0, tiled=True)
+        inner = jnp.dot(normed, full_in, preferred_element_type=jnp.float32)
+        hidden = jnp.maximum(inner, 0.0).astype(jnp.bfloat16)
+        partial_out = jnp.dot(
+            hidden,
+            lax.all_gather(ffn_out, "seq", axis=1, tiled=True),
+            preferred_element_type=jnp.float32,
+        )
     my_lengths = lax.dynamic_index_in_dim(sent_lengths, my_group, 0, keepdims=False)
     my_targets = lax.dynamic_index_in_dim(group_table, my_group, 0, keepdims=False)
     my_starts = jnp.cumsum(my_lengths) - my_lengths
@@ -62,8 +380,9 @@
     for layer_index in range(LAYERS):
         weight_list.append(w_key[layer_index])
         weight_list.append(w_value[layer_index])
-    enc_share = lax.psum_scatter(partial_out, "mp", scatter_dimension=1, tiled=True)
-    encoded = enc_rows.astype(jnp.float32) + enc_share
+    if not fast:
+        enc_share = lax.psum_scatter(partial_out, "mp", scatter_dimension=1, tiled=True)
+        encoded = enc_rows.astype(jnp.float32) + enc_share
     squares = lax.psum(jnp.sum(encoded * encoded, axis=1), "mp")
     gain_part = lax.dynamic_slice_in_dim(final_gain, col_start, col_width, 0)
     memory = (encoded * lax.rsqrt(squares / D + epsilon)[:, None] * gain_part).astype(jnp.bfloat16)

time: 799 us -> 395 us (0.49)
  waiting for transfers between devices: 670 us -> 70.7 us
  Pallas kernels: 0 us -> 221 us
  matrix products: 46.5 us -> 30.4 us
  blocking collectives: 55.6 us -> 43.3 us
    all_gather x2 -> x0, waiting for transfers between devices: 565 us -> none  [the longest x1 287 us: shards(): full_in = lax.all_gather(ffn_in, 'seq', axis=0, tiled=True)]
    pallas_call x0 -> x1, Pallas kernels: none -> 221 us  [ffn_fast(): pl.pallas_call(functools.partial(ffn_kernel, n_seq, n_mp), out_shape=jax....]
    reduce_scatter x1 -> x0, waiting for transfers between devices: 33.1 us -> none  [shards(): lax.psum_scatter(partial_out, 'mp', scatter_dimension=1, tiled=True)]
    dot_general x1 -> x0, matrix products: 16.1 us -> none  [shards(): jnp.dot(hidden, lax.all_gather(ffn_out, 'seq', axis=1, tiled=True), prefe...]
    all_gather x1 -> x0, blocking collectives: 11.5 us -> none  [shards(): whole_rows = lax.all_gather(enc_rows, 'mp', axis=1, tiled=True)]
    unnamed x8 -> x5, waiting for transfers between devices: 64.7 us -> 63.1 us
  transfers between devices with their start and end apart: 6 -> 3, of which waited for: 6 -> 3; matrix products, arithmetic and copies ran while one was open for 1% -> 2% of each run, Pallas kernels for 0% -> 0%
where the time goes in v1:
time: 395 us
  Pallas kernels  221 us (56%)
  waiting for transfers between devices  70.7 us (18%)
  blocking collectives  43.3 us (11%)
  matrix products  30.4 us (8%)
  between operations  13.4 us (3%)
  local copies, waits for them, and re-layouts  11.3 us (3%)
    pallas_call x1, Pallas kernels, ffn_fast(): pl.pallas_call(functools.partial(ffn_kernel, n_seq, n_mp), out_shape=jax....  221 us
    unnamed x5, waiting for transfers between devices  63.1 us
    all_gather x2, blocking collectives, shards(): lax.all_gather(final_state.astype(jnp.bfloat16), 'mp', axis=1, tiled=True)  20.5 us
    psum x1, blocking collectives, shards(): squares = lax.psum(jnp.sum(encoded * encoded, axis=1), 'mp')  13.9 us
    dot_general x4, matrix products, shards(): jnp.einsum('std,de->ste', gathered, weight_matrix, preferred_element_type...  10.8 us
    all_to_all x1, blocking collectives, shards(): lax.all_to_all(blocks, 'seq', split_axis=0, concat_axis=0, tiled=True)  8.96 us
    dot_general x2, matrix products, shards(): jnp.einsum('shqt,sthd->sqhd', weights, value_heads, preferred_element_typ...  8.43 us
  transfers between devices with their start and end apart: 3, of which 3 were waited for; matrix products, arithmetic and copies ran while one was open for 2% of the time, Pallas kernels for 0%

profile of v1, /device:TPU:0, one launch (start us, length us, event | category | flops | bytes accessed | tf_op | source)
XLA Modules:
  0.0 394.6 jit_solution(3669406806014520343)
XLA Ops:
  6.5 0.7 constant_dynamic-slice_fusion
  7.2 0.2 reduce-window_clone.1
  7.4 0.7 subtract_bitcast_fusion
  8.1 0.1 select_reduce_fusion.1
  8.2 0.1 fusion.109
  8.3 2.2 copy-done
  10.5 0.8 copy-done.1
  11.3 0.7 copy-done.2
  12.0 221.3 %shard_map.127 = f32[256,128]{1,0:T(8,128)S(1)} custom-call(bf16[256,128]{1,0:T(8,128)(2,1)S(1)} %copy-done.1, f32[1,1024]{1,0:T(1,128)S(1)} %bitcast.124, bf16[256,8192]{1,0:T(8,128)(2,1)S(1)} %copy-done, bf16[8192,256]{1,0:T(8,128)(2,1)} %fout_ref.1), custom_call_target="tpu_custom_call" | custom-call | tf_op jit(solution)/shard_map/pallas_call | solution.py:280
  233.4 0.1 multiply_reduce_fusion
  233.5 13.9 %psum.7 = f32[256]{0:T(256)S(1)} all-reduce(f32[256]{0:T(256)S(1)} %multiply_reduce_fusion), channel_id=1, replica_groups=mesh['seq'=4,'mp'=8] {'mp'}, use_global_device_ids=true, to_apply=%region_1.2 | all-reduce | flops 256 | bytes 2048 | tf_op jit(solution)/shard_map/psum | solution.py:386
  247.4 0.8 dynamic_slice.10
  248.1 0.1 multiply_convert_fusion
  248.3 1.3 gather_fusion
  249.6 9.0 %all_to_all.5 = bf16[4,128,128]{2,1,0:T(8,128)(2,1)} all-to-all(bf16[4,128,128]{2,1,0:T(8,128)(2,1)S(1)} %bitcast.129), channel_id=1, replica_groups=mesh['seq'=4,'mp'=8] {'seq'}, dimensions={0} | all-to-all | bytes 262144 | tf_op jit(solution)/shard_map/all_to_all | solution.py:391
  258.7 10.6 %all_gather.10 = bf16[256,1024]{1,0:T(8,128)(2,1)S(1)} all-gather(bf16[256,128]{1,0:T(8,128)(2,1)S(1)} %copy-done.3), channel_id=1, replica_groups=mesh['seq'=4,'mp'=8] {'mp'}, dimensions={1}, use_global_device_ids=true | all-gather | bytes 589824 | tf_op jit(solution)/shard_map/all_gather | solution.py:409
  269.2 0.2 fusion.80
  269.4 2.4 fusion.72
  271.8 0.1 copy.44
  272.0 0.1 select_reduce_fusion
  272.1 0.1 iota_compare_fusion
  272.1 7.7 %all-gather.2.cloned.1.call-done = bf16[4,128,1024]{2,1,0:T(8,128)(2,1)} async-done(((bf16[4,128,128]{2,1,0:T(8,128)(2,1)}), bf16[4,128,1024]{2,1,0:T(8,128)(2,1)}) %all-gather.2.cloned.1.call-update) | async-done | bytes 1048592 | tf_op jit(solution)/shard_map/all_gather | solution.py:390
  279.8 3.3 fusion.48
  283.1 0.8 convolution_select_fusion.1
  283.9 0.6 fusion.113
  284.6 2.3 fusion.51
  286.8 4.8 %fusion.78 = bf16[4,64,8,128]{3,1,2,0:T(8,128)(2,1)S(1)} fusion(bf16[4,16,8,8,128]{4,3,2,1,0:T(8,128)(2,1)} %fusion.51, f32[4,8,64]{2,1,0:T(8,128)S(1)} %fusion.113, f32[4,8,64,128]{3,2,1,0:T(8,128)S(1)} %convolution_select_fusion.1), kind=kOutput, calls=%fused_computation.55 | convolution fusion | flops 68159616 | bytes 2629632 | tf_op jit(solution)/shard_map/shqt,sthd->sqhd/dot_general | solution.py:427
  291.7 0.3 copy.31
  292.0 2.3 fusion.60
  294.3 1.0 copy.36
  295.4 0.2 reduce-scatter.9.cloned.1.call-start
  295.6 3.0 fusion.42
  298.7 2.3 fusion.45
  300.9 28.7 %reduce-scatter.7.cloned.1.call-done = bf16[128,256]{1,0:T(8,128)(2,1)} async-done(((bf16[1024,256]{1,0:T(8,128)(2,1)}), bf16[128,256]{1,0:T(8,128)(2,1)}) %reduce-scatter.7.cloned.1.call-update) | async-done | bytes 65552
  329.7 0.9 copy.37
  330.7 9.9 %all_gather.11 = bf16[256,1024]{1,0:T(8,128)(2,1)S(1)} all-gather(bf16[256,128]{1,0:T(8,128)(2,1)S(1)} %fusion.108), channel_id=1, replica_groups=mesh['seq'=4,'mp'=8] {'mp'}, dimensions={1}, use_global_device_ids=true | all-gather | bytes 589824 | tf_op jit(solution)/shard_map/all_gather | solution.py:409
  340.6 0.2 fusion.83
  340.8 2.5 fusion.75
  343.3 0.1 copy.46
  343.4 0.8 convolution_select_fusion
  344.2 0.6 fusion.114
  344.8 3.6 fusion.79
  348.4 0.3 copy.35
  348.8 2.3 fusion.63
  351.1 1.0 copy.38
  352.1 34.3 %reduce-scatter.9.cloned.1.call-done = bf16[128,256]{1,0:T(8,128)(2,1)} async-done(((bf16[1024,256]{1,0:T(8,128)(2,1)}), bf16[128,256]{1,0:T(8,128)(2,1)}) %reduce-scatter.9.cloned.1.call-update) | async-done | bytes 65552
  386.4 0.9 copy.39
  387.4 0.7 add_convert_fusion
  (30 shorter events, 0.2 us)
Async XLA Ops:
  6.5 273.3 %all-gather.2.cloned.1.call-start = ((), (), s32[]{:S(2)}) async-start(), calls=%async_computation.3 | async-start | bytes 1179648 | tf_op jit(solution)/shard_map/all_gather | solution.py:390
  8.3 2.2 copy-start
  10.5 0.8 copy-start.1
  11.3 0.7 copy-start.2
  12.0 246.6 %copy-start.3 = (bf16[256,128]{1,0:T(8,128)(2,1)S(1)}, bf16[256,128]{1,0:T(8,128)(2,1)}, u32[]{:S(2)}) copy-start(bf16[256,128]{1,0:T(8,128)(2,1)} %param.20) | copy-start | bytes 196612
  12.0 257.4 %copy-start.4 = (f32[2,1024]{1,0:T(2,128)S(1)}, f32[2,1024]{1,0:T(2,128)}, u32[]{:S(2)}) copy-start(f32[2,1024]{1,0:T(2,128)} %param.21) | copy-start | bytes 24580
  248.2 23.7 %copy-start.5 = (s32[4,4]{1,0:T(4,128)S(1)}, s32[4,4]{1,0:T(4,128)}, u32[]{:S(2)}) copy-start(s32[4,4]{1,0:T(4,128)} %param.18) | copy-start | bytes 196
  248.3 23.7 %copy-start.6 = (s32[4,4]{1,0:T(4,128)S(1)}, s32[4,4]{1,0:T(4,128)}, u32[]{:S(2)}) copy-start(s32[4,4]{1,0:T(4,128)} %param.19) | copy-start | bytes 196
  258.6 71.1 %reduce-scatter.7.cloned.1.call-start = ((), (), s32[]{:S(2)}) async-start(), calls=%async_computation.4 | async-start | bytes 589824
  279.8 4.8 %copy-start.7 = (bf16[2,1024,1024]{2,1,0:T(8,128)(2,1)S(1)}, bf16[2,1024,1024]{2,1,0:T(8,128)(2,1)}, u32[]{:S(2)}) copy-start(bf16[2,1024,1024]{2,1,0:T(8,128)(2,1)} %param.24) | copy-start | bytes 12582916
  279.8 4.8 %copy-start.9 = (bf16[4,128,1024]{2,1,0:T(8,128)(2,1)S(1)}, bf16[4,128,1024]{2,1,0:T(8,128)(2,1)}, u32[]{:S(2)}) copy-start(bf16[4,128,1024]{2,1,0:T(8,128)(2,1)} %all-gather.2.cloned.1.call-done) | copy-start | bytes 3145732
  295.4 91.0 %reduce-scatter.9.cloned.1.call-start = ((), (), s32[]{:S(2)}) async-start(), calls=%async_computation.5 | async-start | bytes 589824
  295.6 3.0 copy-start.8
  340.8 4.0 %copy-start.10 = (bf16[4,16,8,8,128]{4,3,2,1,0:T(8,128)(2,1)S(1)}, bf16[4,16,8,8,128]{4,3,2,1,0:T(8,128)(2,1)}, u32[]{:S(2)}) copy-start(bf16[4,16,8,8,128]{4,3,2,1,0:T(8,128)(2,1)} %fusion.45) | copy-start | bytes 3145732
Sparse Core Ops, SparseCore 0:
  258.7 21.0 all-gather.1
  295.5 34.1 reduce-scatter.6
  352.3 34.1 reduce-scatter.8

commit v2 on v1

--- a/solution.py
+++ b/solution.py
@@ -39,9 +39,18 @@
     n_mp,
     enc_ref,
     gain_ref,
+    final_gain_ref,
+    sel_ref,
+    mask_ref,
+    dec_ref,
+    dec_gain_ref,
     fin_ref,
     fout_ref,
-    share_ref,
+    wq_ref,
+    wk_ref,
+    wv_ref,
+    wo_ref,
+    out_ref,
     enc_all,
     normed,
     win,
@@ -64,6 +73,31 @@
     red_zs,
     red_zr,
     local_sem,
+    wq,
+    wk,
+    wv,
+    wo,
+    w_sem,
+    dec_all,
+    dec_normed,
+    queries,
+    enc_half,
+    slot_out,
+    slots,
+    memory,
+    keys,
+    values,
+    attended,
+    att_out,
+    att_in,
+    dec_ps,
+    dec_pr,
+    slot_zs,
+    slot_zr,
+    slot_ps,
+    slot_pr,
+    att_ps,
+    att_pr,
 ):
     s = lax.axis_index("seq")
     m = lax.axis_index("mp")
@@ -82,6 +116,154 @@
     pl.semaphore_wait(barrier, n_seq + n_mp - 2)
 
     my_rows = pl.ds(pl.multiple_of(s * rows, rows), rows)
+
+    def plane_gather(buf, send_sem, recv_sem):
+        def copy(slot, bits, peer):
+            return pltpu.make_async_remote_copy(
+                src_ref=buf.at[slot],
+                dst_ref=buf.at[slot],
+                send_sem=send_sem.at[bits],
+                recv_sem=recv_sem.at[bits],
+                device_id=(s, peer),
+                device_id_type=MESH,
+            )
+
+        across = [bits for bits in range(n_mp - 2, 1, -2)]
+        direct = {bits: copy(m, bits, flip(m, bits)) for bits in across + [1]}
+        for bits in across + [1]:
+            direct[bits].start()
+
+        def finish():
+            onward = []
+            for bits in reversed(across):
+                direct[bits].wait_recv()
+                forward = copy(flip(m, bits), bits + 1, flip(m, 1))
+                forward.start()
+                onward.append(forward)
+            direct[1].wait_recv()
+            for forward in onward:
+                forward.wait()
+            for bits in across + [1]:
+                direct[bits].wait_send()
+
+        return finish
+
+    def normalise(buf, dst, count, gain, gain_row):
+        step = min(256, count)
+
+        def body(i, carry):
+            span = pl.ds(pl.multiple_of(i * step, step), step)
+            squares = jnp.zeros((step, 1), jnp.float32)
+            for k in range(n_mp):
+                value = buf[k, span, :].astype(jnp.float32)
+                squares = squares + jnp.sum(value * value, axis=1, keepdims=True)
+            scale = lax.rsqrt(squares / (n_mp * width) + epsilon)
+            for k in range(n_mp):
+                cols = pl.ds(k * width, width)
+                value = buf[k, span, :].astype(jnp.float32)
+                dst[span, cols] = (value * scale * gain[pl.ds(gain_row, 1), cols]).astype(
+                    jnp.bfloat16
+                )
+            return carry
+
+        lax.fori_loop(0, count // step, body, 0)
+
+    def product(left, right, layer, store):
+        columns = right.shape[2]
+        step = min(256, columns)
+
+        def body(i, carry):
+            cols = pl.ds(pl.multiple_of(i * step, step), step)
+            store(
+                cols, jnp.dot(left[...], right[layer, :, cols], preferred_element_type=jnp.float32)
+            )
+            return carry
+
+        lax.fori_loop(0, columns // step, body, 0)
+
+    def project_queries(layer):
+        def store(cols, value):
+            queries[:, cols] = (value * DH ** (-0.5)).astype(jnp.bfloat16)
+
+        product(dec_normed, wq, layer, store)
+
+    def project_memory(layer):
+        def store_key(cols, value):
+            keys[:, cols] = value.astype(jnp.bfloat16)
+
+        def store_value(cols, value):
+            values[:, cols] = value.astype(jnp.bfloat16)
+
+        product(memory, wk, layer, store_key)
+        product(memory, wv, layer, store_value)
+
+    slot_rows = sel_ref.shape[0] // n_seq
+    targets = dec_ref.shape[0]
+    per_sentence = targets // n_seq
+    layers = wq_ref.shape[0]
+    heads = wq_ref.shape[2] // DH
+
+    def attend():
+        def body(i, carry):
+            span = pl.ds(pl.multiple_of(i * per_sentence, per_sentence), per_sentence)
+            slot_span = pl.ds(pl.multiple_of(i * slot_rows, slot_rows), slot_rows)
+            live = mask_ref[i] > 0.5
+            for head in range(heads):
+                cols = pl.ds(head * DH, DH)
+                scores = lax.dot_general(
+                    queries[span, cols],
+                    keys[slot_span, cols],
+                    (((1,), (1,)), ((), ())),
+                    preferred_element_type=jnp.float32,
+                )
+                scores = jnp.where(live, scores, -jnp.inf)
+                top = jnp.max(scores, axis=1, keepdims=True)
+                powers = jnp.exp(scores - top)
+                weights = powers / jnp.sum(powers, axis=1, keepdims=True)
+                attended[span, cols] = jnp.dot(
+                    weights.astype(jnp.bfloat16),
+                    values[slot_span, cols],
+                    preferred_element_type=jnp.float32,
+                ).astype(jnp.bfloat16)
+            return carry
+
+        lax.fori_loop(0, n_seq, body, 0)
+
+    def att_copy(layer, slot, source):
+        return pltpu.make_async_remote_copy(
+            src_ref=att_out.at[layer, slot],
+            dst_ref=att_in.at[layer, source],
+            send_sem=att_ps.at[layer, slot],
+            recv_sem=att_pr.at[layer, source],
+            device_id=(s, slot),
+            device_id_type=MESH,
+        )
+
+    def scatter_output(layer):
+        step = max(width, 256)
+
+        def body(i, carry):
+            cols = pl.ds(pl.multiple_of(i * step, step), step)
+            value = jnp.dot(
+                attended[...], wo[layer, :, cols], preferred_element_type=jnp.float32
+            ).astype(jnp.bfloat16)
+            for j in range(step // width):
+                att_out[layer, i * (step // width) + j] = value[:, j * width : (j + 1) * width]
+            return carry
+
+        lax.fori_loop(0, n_mp * width // step, body, 0)
+        for bits in range(n_mp - 1, 0, -1):
+            att_copy(layer, flip(m, bits), m).start()
+
+    def collect_output(layer):
+        total = att_out[layer, m].astype(jnp.float32)
+        for bits in range(1, n_mp):
+            peer = flip(m, bits)
+            att_copy(layer, peer, peer).wait_recv()
+            total = total + att_in[layer, peer].astype(jnp.float32)
+        for bits in range(1, n_mp):
+            att_copy(layer, flip(m, bits), m).wait_send()
+        return total
 
     own_enc = pltpu.make_async_copy(enc_ref, enc_all.at[m, my_rows], local_sem.at[0])
     own_enc.start()
@@ -133,6 +315,16 @@
         copy.start()
         out_copies.append(copy)
 
+    weight_copies = []
+    for index, (src, dst) in enumerate(((wq_ref, wq), (wk_ref, wk), (wv_ref, wv), (wo_ref, wo))):
+        copy = pltpu.make_async_copy(src, dst, w_sem.at[index])
+        copy.start()
+        weight_copies.append(copy)
+    own_dec = pltpu.make_async_copy(dec_ref, dec_all.at[0, m], local_sem.at[3])
+    own_dec.start()
+    own_dec.wait()
+    finish_dec = plane_gather(dec_all.at[0], dec_ps.at[0], dec_pr.at[0])
+
     own_enc.wait()
     for copy in enc_z:
         copy.wait()
@@ -154,20 +346,13 @@
 
     chunk = min(256, rows)
 
-    def norm_chunk(i, carry):
-        span = pl.ds(pl.multiple_of(i * chunk, chunk), chunk)
-        squares = jnp.zeros((chunk, 1), jnp.float32)
-        for k in range(n_mp):
-            value = enc_all[k, span, :].astype(jnp.float32)
-            squares = squares + jnp.sum(value * value, axis=1, keepdims=True)
-        scale = lax.rsqrt(squares / (n_mp * width) + epsilon)
-        for k in range(n_mp):
-            cols = pl.ds(k * width, width)
-            value = enc_all[k, span, :].astype(jnp.float32)
-            normed[span, cols] = (value * scale * gain_ref[:, cols]).astype(jnp.bfloat16)
-        return carry
-
-    lax.fori_loop(0, total_rows // chunk, norm_chunk, 0)
+    normalise(enc_all, normed, total_rows, gain_ref, 0)
+
+    finish_dec()
+    normalise(dec_all.at[0], dec_normed, targets, dec_gain_ref, 0)
+    for copy in weight_copies:
+        copy.wait()
+    project_queries(0)
 
     own_in.wait()
     for copy in in_copies:
@@ -266,26 +451,83 @@
     for bits, copy in zip(z_order(n_seq), red_z):
         copy.wait()
         total = total + z_in[bits].astype(jnp.float32)
-    share_ref[...] = enc_ref[...].astype(jnp.float32) + total
-
-
-def ffn_fast(enc_rows, ffn_in, ffn_out, enc_gain):
+    enc_half[...] = (enc_ref[...].astype(jnp.float32) + total).astype(jnp.bfloat16)
+
+    def select(group):
+        span = pl.ds(pl.multiple_of(group * slot_rows, slot_rows), slot_rows)
+        return jnp.dot(
+            sel_ref[span, :], enc_half[...], preferred_element_type=jnp.float32
+        ).astype(jnp.bfloat16)
+
+    my_slots = pl.ds(pl.multiple_of(s * slot_rows, slot_rows), slot_rows)
+    slot_z = []
+    for bits in z_order(n_seq):
+        peer = flip(s, bits)
+        slot_out[bits] = select(peer)
+        copy = pltpu.make_async_remote_copy(
+            src_ref=slot_out.at[bits],
+            dst_ref=slots.at[m, my_slots],
+            send_sem=slot_zs.at[bits],
+            recv_sem=slot_zr.at[bits],
+            device_id=(peer, m),
+            device_id_type=MESH,
+        )
+        copy.start()
+        slot_z.append(copy)
+    slots[m, my_slots, :] = select(s)
+    for copy in slot_z:
+        copy.wait()
+
+    plane_gather(slots, slot_ps, slot_pr)()
+    normalise(slots, memory, n_seq * slot_rows, final_gain_ref, 0)
+    project_memory(0)
+
+    state = dec_ref[...].astype(jnp.float32)
+    for layer in range(layers):
+        if layer > 0:
+            dec_all[layer, m] = state.astype(jnp.bfloat16)
+            plane_gather(dec_all.at[layer], dec_ps.at[layer], dec_pr.at[layer])()
+            normalise(dec_all.at[layer], dec_normed, targets, dec_gain_ref, layer)
+            project_queries(layer)
+        attend()
+        scatter_output(layer)
+        if layer + 1 < layers:
+            project_memory(layer + 1)
+        state = state + collect_output(layer)
+    out_ref[...] = state.astype(out_ref.dtype)
+
+
+def whole_fast(
+    enc_rows,
+    ffn_in,
+    ffn_out,
+    enc_gain,
+    final_gain,
+    select_rows,
+    live,
+    dec_rows,
+    dec_gain,
+    w_query,
+    w_key,
+    w_value,
+    w_output,
+):
     n_seq, n_mp = lax.axis_size("seq"), lax.axis_size("mp")
     rows, width = enc_rows.shape
     depth, units = ffn_in.shape[0], ffn_in.shape[1] // n_seq
     out_width = ffn_out.shape[1]
     total = rows * n_seq
     full = width * n_mp
+    targets = dec_rows.shape[0]
+    layers, _, heads_width = w_query.shape
+    slot_total = select_rows.shape[0]
+    half = jnp.bfloat16
     dma = pltpu.SemaphoreType.DMA
     return pl.pallas_call(
         functools.partial(ffn_kernel, n_seq, n_mp),
-        out_shape=jax.ShapeDtypeStruct((rows, width), jnp.float32),
-        in_specs=[
-            pl.BlockSpec(memory_space=pltpu.VMEM),
-            pl.BlockSpec(memory_space=pltpu.VMEM),
-            pl.BlockSpec(memory_space=pl.ANY),
-            pl.BlockSpec(memory_space=pl.ANY),
-        ],
+        out_shape=jax.ShapeDtypeStruct(dec_rows.shape, dec_rows.dtype),
+        in_specs=[pl.BlockSpec(memory_space=pltpu.VMEM)] * 7
+        + [pl.BlockSpec(memory_space=pl.ANY)] * 6,
         out_specs=pl.BlockSpec(memory_space=pltpu.VMEM),
         scratch_shapes=[
             pltpu.VMEM((n_mp, total, width), jnp.bfloat16),
@@ -309,15 +551,54 @@
             dma((n_mp,)),
             dma((n_seq,)),
             dma((n_seq,)),
-            dma((3,)),
+            dma((4,)),
+            pltpu.VMEM(w_query.shape, half),
+            pltpu.VMEM(w_key.shape, half),
+            pltpu.VMEM(w_value.shape, half),
+            pltpu.VMEM(w_output.shape, half),
+            dma((4,)),
+            pltpu.VMEM((layers, n_mp, targets, width), half),
+            pltpu.VMEM((targets, full), half),
+            pltpu.VMEM((targets, heads_width), half),
+            pltpu.VMEM((rows, width), half),
+            pltpu.VMEM((n_seq, slot_total // n_seq, width), half),
+            pltpu.VMEM((n_mp, slot_total, width), half),
+            pltpu.VMEM((slot_total, full), half),
+            pltpu.VMEM((slot_total, heads_width), half),
+            pltpu.VMEM((slot_total, heads_width), half),
+            pltpu.VMEM((targets, heads_width), half),
+            pltpu.VMEM((layers, n_mp, targets, width), half),
+            pltpu.VMEM((layers, n_mp, targets, width), half),
+            dma((layers, n_mp)),
+            dma((layers, n_mp)),
+            dma((n_seq,)),
+            dma((n_seq,)),
+            dma((n_mp,)),
+            dma((n_mp,)),
+            dma((layers, n_mp)),
+            dma((layers, n_mp)),
         ],
         compiler_params=pltpu.CompilerParams(
-            collective_id=0, has_side_effects=True, vmem_limit_bytes=48 * 1024 * 1024
+            collective_id=0, has_side_effects=True, vmem_limit_bytes=60 * 1024 * 1024
         ),
-    )(enc_rows, enc_gain.reshape(1, full), ffn_in, ffn_out)
-
-
-def fast_shapes(enc_rows, ffn_in, ffn_out):
+    )(
+        enc_rows,
+        enc_gain.reshape(1, full),
+        final_gain.reshape(1, full),
+        select_rows,
+        live,
+        dec_rows,
+        dec_gain,
+        ffn_in,
+        ffn_out,
+        w_query,
+        w_key,
+        w_value,
+        w_output,
+    )
+
+
+def fast_shapes(enc_rows, ffn_in, ffn_out, dec_rows, w_query):
     n_seq, n_mp = lax.axis_size("seq"), lax.axis_size("mp")
     power = (n_seq & (n_seq - 1)) == 0 and (n_mp & (n_mp - 1)) == 0
     aligned = (
@@ -326,6 +607,10 @@
         and (ffn_in.shape[1] // n_seq) % 256 == 0
         and ffn_out.shape[1] % enc_rows.shape[1] == 0
         and enc_rows.shape[0] % 256 == 0
+        and dec_rows.shape[0] % 256 == 0
+        and (2 * enc_rows.shape[0] // n_seq) % 128 == 0
+        and w_query.shape[2] % 256 == 0
+        and w_query.shape[1] % 256 == 0
     )
     return power and aligned
 
@@ -351,10 +636,8 @@
     col_start = lax.axis_index("mp") * col_width
     row_count = enc_rows.shape[0]
     max_length = 2 * row_count // group_count
-    fast = fast_shapes(enc_rows, ffn_in, ffn_out)
-    if fast:
-        encoded = ffn_fast(enc_rows, ffn_in, ffn_out, enc_gain)
-    else:
+    fast = fast_shapes(enc_rows, ffn_in, ffn_out, dec_rows, w_query)
+    if not fast:
         whole_rows = lax.all_gather(enc_rows, "mp", axis=1, tiled=True)
         normed = rms_scale(whole_rows.astype(jnp.float32), enc_gain).astype(jnp.bfloat16)
         full_in = lax.all_gather(ffn_in, "seq", axis=0, tiled=True)
@@ -375,14 +658,30 @@
     row_index = jnp.minimum(send_starts[:, None] + positions[None, :], row_count - 1)
     recv_lengths = jnp.sum(jnp.where(group_table == my_group, sent_lengths, 0), axis=1)
     live_mask = positions[None, :] < recv_lengths[:, None]
+    if fast:
+        select_rows = row_index.reshape(-1, 1) == jnp.arange(row_count, dtype=jnp.int32)[None, :]
+        return whole_fast(
+            enc_rows,
+            ffn_in,
+            ffn_out,
+            enc_gain,
+            final_gain,
+            select_rows.astype(jnp.bfloat16),
+            live_mask[:, None, :].astype(jnp.float32),
+            dec_rows,
+            dec_gain,
+            w_query,
+            w_key,
+            w_value,
+            w_output,
+        )
     kv_width = w_key.shape[2]
     weight_list = []
     for layer_index in range(LAYERS):
         weight_list.append(w_key[layer_index])
         weight_list.append(w_value[layer_index])
-    if not fast:
-        enc_share = lax.psum_scatter(partial_out, "mp", scatter_dimension=1, tiled=True)
-        encoded = enc_rows.astype(jnp.float32) + enc_share
+    enc_share = lax.psum_scatter(partial_out, "mp", scatter_dimension=1, tiled=True)
+    encoded = enc_rows.astype(jnp.float32) + enc_share
     squares = lax.psum(jnp.sum(encoded * encoded, axis=1), "mp")
     gain_part = lax.dynamic_slice_in_dim(final_gain, col_start, col_width, 0)
     memory = (encoded * lax.rsqrt(squares / D + epsilon)[:, None] * gain_part).astype(jnp.bfloat16)

time: 395 us -> 295 us (0.75)
  waiting for transfers between devices: 70.7 us -> 0 us
  Pallas kernels: 221 us -> 289 us
  blocking collectives: 43.3 us -> 0 us
  matrix products: 30.4 us -> 0 us
  between operations: 13.4 us -> 0.01 us
  local copies, waits for them, and re-layouts: 11.3 us -> 2.16 us
    pallas_call x1, Pallas kernels: 221 us -> 289 us  [whole_fast(): pl.pallas_call(functools.partial(ffn_kernel, n_seq, n_mp), out_shape=jax....]
    unnamed x5 -> x0, waiting for transfers between devices: 63.1 us -> none
    dot_general x12 -> x0, matrix products: 30.4 us -> none  [the longest x4 10.8 us: shards(): jnp.einsum('std,de->ste', gathered, weight_matrix, preferred_element_type...]
    all_gather x2 -> x0, blocking collectives: 20.5 us -> none  [shards(): lax.all_gather(final_state.astype(jnp.bfloat16), 'mp', axis=1, tiled=True)]
    psum x1 -> x0, blocking collectives: 13.9 us -> none  [shards(): squares = lax.psum(jnp.sum(encoded * encoded, axis=1), 'mp')]
    all_to_all x1 -> x0, blocking collectives: 8.96 us -> none  [shards(): lax.all_to_all(blocks, 'seq', split_axis=0, concat_axis=0, tiled=True)]
    all_gather x1 -> x0, waiting for transfers between devices: 7.65 us -> none  [shards(): lax.all_gather(lax.all_to_all(blocks, 'seq', split_axis=0, concat_axis=0,...]
    unnamed x28 -> x1, local copies, waits for them, and re-layouts: 7.85 us -> 1.47 us
  transfers between devices with their start and end apart: 3 -> 0, of which waited for: 3 -> 0; matrix products, arithmetic and copies ran while one was open for 2% -> 0% of each run, Pallas kernels for 0% -> 0%
where the time goes in v2:
time: 295 us; the launch traced here: 294 us
  Pallas kernels  289 us (98%)
  other arithmetic  3.37 us (1%)
    pallas_call x1, Pallas kernels, whole_fast(): pl.pallas_call(functools.partial(ffn_kernel, n_seq, n_mp), out_shape=jax....  289 us

profile of v2, /device:TPU:0, one launch (start us, length us, event | category | flops | bytes accessed | tf_op | source)
XLA Modules:
  0.0 294.5 jit_solution(3009852081508926711)
XLA Ops:
  0.0 0.8 select_reduce_fusion
  0.8 0.7 constant_dynamic-slice_fusion
  1.5 0.2 reduce-window_clone.1
  1.7 0.7 subtract_bitcast_fusion
  2.4 0.1 select_reduce_fusion.1
  2.5 0.1 minimum_bitcast_fusion
  2.6 0.7 compare_convert_fusion.mask_ref
  3.2 0.8 fusion.sel_ref
  4.1 288.9 %shard_map.127 = bf16[256,128]{1,0:T(8,128)(2,1)} custom-call(bf16[256,128]{1,0:T(8,128)(2,1)} %enc_ref.1, f32[1,1024]{1,0:T(1,128)} %bitcast.8, f32[1,1024]{1,0:T(1,128)} %bitcast.9, bf16[512,256]{1,0:T(8,128)(2,1)} %fusion.sel_ref, f32[4,1,128]{2,1,0:T(1,128)} %compare_convert_fusion.mask_ref, bf16[256,128]{1,0:T(8,128)(2,1)} %dec_ref.1, ...), custom_call_target="tpu_custom_call" | custom-call | tf_op jit(solution)/shard_map/pallas_call | solution.py:526
  293.0 1.5 copy.15

commit v3 on v2

--- a/solution.py
+++ b/solution.py
@@ -40,8 +40,8 @@
     enc_ref,
     gain_ref,
     final_gain_ref,
-    sel_ref,
-    mask_ref,
+    lengths_ref,
+    table_ref,
     dec_ref,
     dec_gain_ref,
     fin_ref,
@@ -98,6 +98,9 @@
     slot_pr,
     att_ps,
     att_pr,
+    sel,
+    mask,
+    own_out_sem,
 ):
     s = lax.axis_index("seq")
     m = lax.axis_index("mp")
@@ -197,7 +200,7 @@
         product(memory, wk, layer, store_key)
         product(memory, wv, layer, store_value)
 
-    slot_rows = sel_ref.shape[0] // n_seq
+    slot_rows = sel.shape[0] // n_seq
     targets = dec_ref.shape[0]
     per_sentence = targets // n_seq
     layers = wq_ref.shape[0]
@@ -207,23 +210,25 @@
         def body(i, carry):
             span = pl.ds(pl.multiple_of(i * per_sentence, per_sentence), per_sentence)
             slot_span = pl.ds(pl.multiple_of(i * slot_rows, slot_rows), slot_rows)
-            live = mask_ref[i] > 0.5
-            for head in range(heads):
-                cols = pl.ds(head * DH, DH)
-                scores = lax.dot_general(
+            live = mask[i] > 0.5
+            columns = [pl.ds(head * DH, DH) for head in range(heads)]
+            scores = [
+                lax.dot_general(
                     queries[span, cols],
                     keys[slot_span, cols],
                     (((1,), (1,)), ((), ())),
                     preferred_element_type=jnp.float32,
                 )
-                scores = jnp.where(live, scores, -jnp.inf)
-                top = jnp.max(scores, axis=1, keepdims=True)
-                powers = jnp.exp(scores - top)
-                weights = powers / jnp.sum(powers, axis=1, keepdims=True)
+                for cols in columns
+            ]
+            scores = [jnp.where(live, score, -jnp.inf) for score in scores]
+            tops = [jnp.max(score, axis=1, keepdims=True) for score in scores]
+            powers = [jnp.exp(score - top) for score, top in zip(scores, tops)]
+            sums = [jnp.sum(power, axis=1, keepdims=True) for power in powers]
+            weights = [(power / total).astype(jnp.bfloat16) for power, total in zip(powers, sums)]
+            for cols, weight in zip(columns, weights):
                 attended[span, cols] = jnp.dot(
-                    weights.astype(jnp.bfloat16),
-                    values[slot_span, cols],
-                    preferred_element_type=jnp.float32,
+                    weight, values[slot_span, cols], preferred_element_type=jnp.float32
                 ).astype(jnp.bfloat16)
             return carry
 
@@ -284,12 +289,19 @@
         fin_ref.at[:, pl.ds(pl.multiple_of(s * units, units), units)], win.at[s], local_sem.at[1]
     )
     own_in.start()
-    own_out = pltpu.make_async_copy(
-        fout_ref.at[pl.ds(pl.multiple_of(s * units, units), units)], wout.at[s], local_sem.at[2]
-    )
-    own_out.start()
+    own_out = [
+        pltpu.make_async_copy(
+            fout_ref.at[
+                pl.ds(pl.multiple_of(s * units, units), units), pl.ds(j * width, width)
+            ],
+            wout.at[s, j],
+            own_out_sem.at[j],
+        )
+        for j in range(per_block)
+    ]
+    for copy in own_out:
+        copy.start()
     in_copies = []
-    out_copies = []
     for bits in z_order(n_seq):
         peer = flip(s, bits)
         copy = pltpu.make_async_remote_copy(
@@ -302,18 +314,23 @@
         )
         copy.start()
         in_copies.append(copy)
-    for bits in z_order(n_seq):
-        peer = flip(s, bits)
-        copy = pltpu.make_async_remote_copy(
-            src_ref=fout_ref.at[pl.ds(pl.multiple_of(peer * units, units), units)],
-            dst_ref=wout.at[s],
-            send_sem=out_s.at[bits],
-            recv_sem=out_r.at[bits],
+    def out_copy(bits, peer, j):
+        return pltpu.make_async_remote_copy(
+            src_ref=fout_ref.at[
+                pl.ds(pl.multiple_of(peer * units, units), units), pl.ds(j * width, width)
+            ],
+            dst_ref=wout.at[s, j],
+            send_sem=out_s.at[bits, j],
+            recv_sem=out_r.at[bits, j],
             device_id=(peer, m),
             device_id_type=MESH,
         )
-        copy.start()
-        out_copies.append(copy)
+
+    for j in range(per_block):
+        out_copy(1, flip(s, 1), j).start()
+    for j in range(per_block):
+        for bits in range(2, n_seq):
+            out_copy(bits, flip(s, bits), j).start()
 
     weight_copies = []
     for index, (src, dst) in enumerate(((wq_ref, wq), (wk_ref, wk), (wv_ref, wv), (wo_ref, wo))):
@@ -347,6 +364,25 @@
     chunk = min(256, rows)
 
     normalise(enc_all, normed, total_rows, gain_ref, 0)
+
+    for group in range(n_seq):
+        start = jnp.int32(0)
+        before = jnp.int32(0)
+        for j in range(n_seq):
+            start = start + jnp.where(table_ref[s, j] == group, before, 0)
+            before = before + lengths_ref[s, j]
+        position = lax.broadcasted_iota(jnp.int32, (slot_rows, rows), 0)
+        column = lax.broadcasted_iota(jnp.int32, (slot_rows, rows), 1)
+        wanted = jnp.minimum(position + start, rows - 1)
+        sel[pl.ds(group * slot_rows, slot_rows), :] = jnp.where(wanted == column, 1.0, 0.0).astype(
+            jnp.bfloat16
+        )
+    for source in range(n_seq):
+        length = jnp.int32(0)
+        for j in range(n_seq):
+            length = length + jnp.where(table_ref[source, j] == s, lengths_ref[source, j], 0)
+        slot = lax.broadcasted_iota(jnp.int32, (1, slot_rows), 1)
+        mask[source] = jnp.where(slot < length, 1.0, 0.0)
 
     finish_dec()
     normalise(dec_all.at[0], dec_normed, targets, dec_gain_ref, 0)
@@ -375,46 +411,60 @@
 
     lax.fori_loop(0, (total_rows // chunk) * (units // tile), hidden_chunk, 0)
 
-    own_out.wait()
-
-    def out_block(block):
-        def rows_chunk(i, carry):
-            span = pl.ds(pl.multiple_of(i * chunk, chunk), chunk)
-            value = jnp.dot(hidden[span, :], wout[block], preferred_element_type=jnp.float32)
-            for j in range(per_block):
-                part_out[block * per_block + j, span, :] = value[
-                    :, j * width : (j + 1) * width
-                ].astype(jnp.bfloat16)
-            return carry
-
-        lax.fori_loop(0, total_rows // chunk, rows_chunk, 0)
-
-    def send_copy(slot):
+    def send_copy(slot, span):
         return pltpu.make_async_remote_copy(
-            src_ref=part_out.at[slot],
-            dst_ref=part_in.at[m],
+            src_ref=part_out.at[slot, span],
+            dst_ref=part_in.at[m, span],
             send_sem=red_ps.at[slot],
             recv_sem=red_pr.at[m],
             device_id=(s, slot),
             device_id_type=MESH,
         )
 
-    def send_block(block):
-        out_block(block)
-        for j in range(per_block):
-            slot = block * per_block + j
+    def send_block(block, j):
+        slot = block * per_block + j
+
+        def rows_chunk(i, carry):
+            span = pl.ds(pl.multiple_of(i * chunk, chunk), chunk)
+            part_out[slot, span, :] = jnp.dot(
+                hidden[span, :], wout[block, j], preferred_element_type=jnp.float32
+            ).astype(jnp.bfloat16)
 
             @pl.when(slot != m)
             def _():
-                send_copy(slot).start()
-
-    send_block(s)
-    for bits, copy in zip(z_order(n_seq), out_copies):
-        copy.wait()
-        send_block(flip(s, bits))
-
+                send_copy(slot, span).start()
+
+            return carry
+
+        lax.fori_loop(0, total_rows // chunk, rows_chunk, 0)
+
+    def receive_block(bits, j):
+        peer = flip_any(bits)
+        out_copy(bits, peer, j).wait()
+        send_block(peer, j)
+
+    inner = (s % 2 + s // 2) % 2
+
+    def flip_any(bits):
+        if isinstance(bits, int):
+            return flip(s, bits)
+        return flip(s, 2) * (3 - bits) + flip(s, 3) * (bits - 2)
+
+    later = list(range(2, n_seq))
+    if n_seq == 4:
+        later = [2 + inner, 3 - inner]
+    for j in range(per_block):
+        own_out[j].wait()
+        send_block(s, j)
+    for j in range(per_block):
+        receive_block(1, j)
+    for j in range(per_block):
+        for bits in later:
+            receive_block(bits, j)
+
+    everything = pl.ds(0, total_rows)
     for bits in range(1, n_mp):
-        send_copy(flip(m, bits)).wait_send()
+        send_copy(flip(m, bits), everything).wait_send()
     for bits in range(1, n_mp):
         peer = flip(m, bits)
         pltpu.make_async_remote_copy(
@@ -456,7 +506,7 @@
     def select(group):
         span = pl.ds(pl.multiple_of(group * slot_rows, slot_rows), slot_rows)
         return jnp.dot(
-            sel_ref[span, :], enc_half[...], preferred_element_type=jnp.float32
+            sel[span, :], enc_half[...], preferred_element_type=jnp.float32
         ).astype(jnp.bfloat16)
 
     my_slots = pl.ds(pl.multiple_of(s * slot_rows, slot_rows), slot_rows)
@@ -503,8 +553,8 @@
     ffn_out,
     enc_gain,
     final_gain,
-    select_rows,
-    live,
+    sent_lengths,
+    group_table,
     dec_rows,
     dec_gain,
     w_query,
@@ -520,20 +570,23 @@
     full = width * n_mp
     targets = dec_rows.shape[0]
     layers, _, heads_width = w_query.shape
-    slot_total = select_rows.shape[0]
+    slot_total = 2 * rows
+    per_block = out_width // width
     half = jnp.bfloat16
     dma = pltpu.SemaphoreType.DMA
     return pl.pallas_call(
         functools.partial(ffn_kernel, n_seq, n_mp),
         out_shape=jax.ShapeDtypeStruct(dec_rows.shape, dec_rows.dtype),
-        in_specs=[pl.BlockSpec(memory_space=pltpu.VMEM)] * 7
+        in_specs=[pl.BlockSpec(memory_space=pltpu.VMEM)] * 3
+        + [pl.BlockSpec(memory_space=pltpu.SMEM)] * 2
+        + [pl.BlockSpec(memory_space=pltpu.VMEM)] * 2
         + [pl.BlockSpec(memory_space=pl.ANY)] * 6,
         out_specs=pl.BlockSpec(memory_space=pltpu.VMEM),
         scratch_shapes=[
             pltpu.VMEM((n_mp, total, width), jnp.bfloat16),
             pltpu.VMEM((total, full), jnp.bfloat16),
             pltpu.VMEM((n_seq, depth, units), jnp.bfloat16),
-            pltpu.VMEM((n_seq, units, out_width), jnp.bfloat16),
+            pltpu.VMEM((n_seq, per_block, units, width), jnp.bfloat16),
             pltpu.VMEM((total, units), jnp.bfloat16),
             pltpu.VMEM((n_mp, total, width), jnp.bfloat16),
             pltpu.VMEM((n_mp, total, width), jnp.bfloat16),
@@ -545,8 +598,8 @@
             dma((n_mp,)),
             dma((n_seq,)),
             dma((n_seq,)),
-            dma((n_seq,)),
-            dma((n_seq,)),
+            dma((n_seq, per_block)),
+            dma((n_seq, per_block)),
             dma((n_mp,)),
             dma((n_mp,)),
             dma((n_seq,)),
@@ -577,6 +630,9 @@
             dma((n_mp,)),
             dma((layers, n_mp)),
             dma((layers, n_mp)),
+            pltpu.VMEM((slot_total, rows), half),
+            pltpu.VMEM((n_seq, 1, slot_total // n_seq), jnp.float32),
+            dma((per_block,)),
         ],
         compiler_params=pltpu.CompilerParams(
             collective_id=0, has_side_effects=True, vmem_limit_bytes=60 * 1024 * 1024
@@ -585,8 +641,8 @@
         enc_rows,
         enc_gain.reshape(1, full),
         final_gain.reshape(1, full),
-        select_rows,
-        live,
+        sent_lengths,
+        group_table,
         dec_rows,
         dec_gain,
         ffn_in,
@@ -659,15 +715,14 @@
     recv_lengths = jnp.sum(jnp.where(group_table == my_group, sent_lengths, 0), axis=1)
     live_mask = positions[None, :] < recv_lengths[:, None]
     if fast:
-        select_rows = row_index.reshape(-1, 1) == jnp.arange(row_count, dtype=jnp.int32)[None, :]
         return whole_fast(
             enc_rows,
             ffn_in,
             ffn_out,
             enc_gain,
             final_gain,
-            select_rows.astype(jnp.bfloat16),
-            live_mask[:, None, :].astype(jnp.float32),
+            sent_lengths,
+            group_table,
             dec_rows,
             dec_gain,
             w_query,

time: 295 us -> 262 us (0.89)
  Pallas kernels: 289 us -> 260 us
  other arithmetic: 3.37 us -> 0 us
    pallas_call x1, Pallas kernels: 289 us -> 260 us  [whole_fast(): pl.pallas_call(functools.partial(ffn_kernel, n_seq, n_mp), out_shape=jax....]
where the time goes in v3:
time: 262 us; the launch traced here: 261 us
  Pallas kernels  260 us (99%)
    pallas_call x1, Pallas kernels, whole_fast(): pl.pallas_call(functools.partial(ffn_kernel, n_seq, n_mp), out_shape=jax....  260 us

profile of v3, /device:TPU:0, one launch (start us, length us, event | category | flops | bytes accessed | tf_op | source)
XLA Modules:
  0.0 261.3 jit_solution(5203307545334710502)
XLA Ops:
  0.0 259.8 %shard_map.127 = bf16[256,128]{1,0:T(8,128)(2,1)} custom-call(bf16[256,128]{1,0:T(8,128)(2,1)} %enc_ref.1, f32[1,1024]{1,0:T(1,128)} %bitcast.2, f32[1,1024]{1,0:T(1,128)} %bitcast.3, s32[4,4]{1,0:T(4,128)} %lengths_ref.1, s32[4,4]{1,0:T(4,128)} %table_ref.1, bf16[256,128]{1,0:T(8,128)(2,1)} %dec_ref.1, f32[2,1024]{1,0:T(2,128)} %dec_gain_ref.1, ...), custom_call_target="tpu_custom_call" | custom-call | tf_op jit(solution)/shard_map/pallas_call | solution.py:577
  259.8 1.5 copy.15

commit v4 on v3

--- a/solution.py
+++ b/solution.py
@@ -232,7 +232,7 @@
                 ).astype(jnp.bfloat16)
             return carry
 
-        lax.fori_loop(0, n_seq, body, 0)
+        lax.fori_loop(0, n_seq, body, 0, unroll=n_seq <= 4)
 
     def att_copy(layer, slot, source):
         return pltpu.make_async_remote_copy(
@@ -248,17 +248,22 @@
         step = max(width, 256)
 
         def body(i, carry):
-            cols = pl.ds(pl.multiple_of(i * step, step), step)
+            chip = (i + m // (step // width) + 1) % (n_mp * width // step)
+            cols = pl.ds(pl.multiple_of(chip * step, step), step)
             value = jnp.dot(
                 attended[...], wo[layer, :, cols], preferred_element_type=jnp.float32
             ).astype(jnp.bfloat16)
             for j in range(step // width):
-                att_out[layer, i * (step // width) + j] = value[:, j * width : (j + 1) * width]
+                slot = chip * (step // width) + j
+                att_out[layer, slot] = value[:, j * width : (j + 1) * width]
+
+                @pl.when(slot != m)
+                def _():
+                    att_copy(layer, slot, m).start()
+
             return carry
 
         lax.fori_loop(0, n_mp * width // step, body, 0)
-        for bits in range(n_mp - 1, 0, -1):
-            att_copy(layer, flip(m, bits), m).start()
 
     def collect_output(layer):
         total = att_out[layer, m].astype(jnp.float32)

time: 262 us -> 258 us (0.985)
  Pallas kernels: 260 us -> 256 us
    pallas_call x1, Pallas kernels: 260 us -> 256 us  [whole_fast(): pl.pallas_call(functools.partial(ffn_kernel, n_seq, n_mp), out_shape=jax....]
where the time goes in v4:
time: 258 us
  Pallas kernels  256 us (99%)
    pallas_call x1, Pallas kernels, whole_fast(): pl.pallas_call(functools.partial(ffn_kernel, n_seq, n_mp), out_shape=jax....  256 us

profile of v4, /device:TPU:0, one launch (start us, length us, event | category | flops | bytes accessed | tf_op | source)
XLA Modules:
  0.0 257.5 jit_solution(8070180594872550948)
XLA Ops:
  0.0 256.0 %shard_map.127 = bf16[256,128]{1,0:T(8,128)(2,1)} custom-call(bf16[256,128]{1,0:T(8,128)(2,1)} %enc_ref.1, f32[1,1024]{1,0:T(1,128)} %bitcast.2, f32[1,1024]{1,0:T(1,128)} %bitcast.3, s32[4,4]{1,0:T(4,128)} %lengths_ref.1, s32[4,4]{1,0:T(4,128)} %table_ref.1, bf16[256,128]{1,0:T(8,128)(2,1)} %dec_ref.1, f32[2,1024]{1,0:T(2,128)} %dec_gain_ref.1, ...), custom_call_target="tpu_custom_call" | custom-call | tf_op jit(solution)/shard_map/pallas_call | solution.py:582
  256.0 1.5 copy.15
